TPU v7x, 256 devices: a whole 4x4x8 slice. The times are simulated.
256 devices in a mesh: row: 16 (over y_lo, x, core), col: 16 (over z, y_hi).
Axes of the slice: x: 4, y: 4 (y_hi: 2, y_lo: 2; y = y_hi * 2 + y_lo), z: 8, core: 2. Of those that a mesh axis runs over, the one named last changes fastest.
Arguments:
- counts: int32 [16, 16, 6, 8, 128, 128], P('row', 'col'), may hold values from 0 to 5
- block_coords: int32 [3, 16, 16, 6], P(None, 'row', 'col'), may hold values from 0 to 127, as said below
- block_count: int32 [16, 16], P('row', 'col'), may hold values from 1 to 6, as said below
- factor_a: float32 [32768, 128], P(('row', 'col')), may hold values from -0.6 to 0.6
- factor_b: float32 [32768, 128], P(('col', 'row')), may hold values from -0.6 to 0.6
- factor_c: float32 [1024, 128], replicated, may hold values from -0.6 to 0.6
Outputs:
- updated_a: float32 [32768, 128], P(('row', 'col'))
- updated_b: float32 [32768, 128], P(('col', 'row'))
Inputs may be any that keep to these rules, and one draw needn't show every extreme that they name: `block_coords`: the slots of one cell name distinct blocks; the first index is below 16, the second below 16, the third below 128. `block_count`: at least one cell has all 6 slots live in every draw.
All inputs are finite; a program needn't handle non-finite values.
Results may differ from a plain program's by a relative error of at most 0.0003.
Values sent between devices are 32-bit elements; how exact they have to be, the bound alone decides.
No kernel may reach another device: no remote copies, remote signals or barrier semaphores. Data moves between devices by JAX's collectives and lax.ppermute only.
A program may use at most 64 MiB of HBM per device.

v0:
```python
import jax
import jax.numpy as jnp
from jax import lax
from jax.sharding import PartitionSpec as P

STEPS = 2
step_rate = 0.004
highest = lax.Precision.HIGHEST


def block_gradient(piece_a, piece_b, piece_c, observed, valid_flag):
    depth = piece_c.shape[0]
    side = piece_a.shape[0]
    rank = piece_a.shape[1]
    scaled_a = (piece_c[:, None, :] * piece_a[None, :, :]).reshape(depth * side, rank)
    model = jnp.dot(scaled_a, piece_b.T, precision=highest, preferred_element_type=jnp.float32)
    residual = (
        jnp.exp(model) - observed.reshape(depth * side, side).astype(jnp.float32)
    ) * valid_flag
    scaled_b = piece_c[:, None, :] * piece_b[None, :, :]
    grad_a = jnp.einsum(
        "kab,kbr->ar", residual.reshape(depth, side, side), scaled_b, precision=highest
    )
    grad_b = jnp.dot(residual.T, scaled_a, precision=highest, preferred_element_type=jnp.float32)
    return (grad_a, grad_b)


def local_gradients(band_a, band_b, factor_c, counts, block_coords, block_count):
    slot_total = counts.shape[2]
    depth = counts.shape[3]
    side = counts.shape[4]
    limit = block_count[0, 0]

    def visit_slot(partial_value, slot_index):
        grad_a, grad_b = partial_value
        start_a = block_coords[0, 0, 0, slot_index] * side
        start_b = block_coords[1, 0, 0, slot_index] * side
        start_c = block_coords[2, 0, 0, slot_index] * depth
        valid_flag = (slot_index < limit).astype(jnp.float32)
        piece_a = lax.dynamic_slice_in_dim(band_a, start_a, side, 0)
        piece_b = lax.dynamic_slice_in_dim(band_b, start_b, side, 0)
        piece_c = lax.dynamic_slice_in_dim(factor_c, start_c, depth, 0)
        observed = counts[0, 0, slot_index]
        block_a, block_b = block_gradient(piece_a, piece_b, piece_c, observed, valid_flag)
        old_a = lax.dynamic_slice_in_dim(grad_a, start_a, side, 0)
        old_b = lax.dynamic_slice_in_dim(grad_b, start_b, side, 0)
        grad_a = lax.dynamic_update_slice_in_dim(grad_a, old_a + block_a, start_a, 0)
        grad_b = lax.dynamic_update_slice_in_dim(grad_b, old_b + block_b, start_b, 0)
        return ((grad_a, grad_b), None)

    start = (jnp.zeros_like(band_a), jnp.zeros_like(band_b))
    result, unused = lax.scan(visit_slot, start, jnp.arange(slot_total, dtype=jnp.int32))
    return result


def local(counts, block_coords, block_count, factor_a, factor_b, factor_c):
    for step_index in range(STEPS):
        band_a = lax.all_gather(factor_a, "col", axis=0, tiled=True)
        band_b = lax.all_gather(factor_b, "row", axis=0, tiled=True)
        grad_a, grad_b = local_gradients(
            band_a, band_b, factor_c, counts, block_coords, block_count
        )
        share_a = lax.psum_scatter(grad_a, "col", scatter_dimension=0, tiled=True)
        share_b = lax.psum_scatter(grad_b, "row", scatter_dimension=0, tiled=True)
        factor_a = factor_a - step_rate * share_a
        factor_b = factor_b - step_rate * share_b
    return (factor_a, factor_b)


def solution(mesh):
    return jax.shard_map(
        local,
        mesh=mesh,
        in_specs=(
            P("row", "col", None, None, None, None),
            P(None, "row", "col", None),
            P("row", "col"),
            P(("row", "col"), None),
            P(("col", "row"), None),
            P(),
        ),
        out_specs=(P(("row", "col"), None), P(("col", "row"), None)),
        check_vma=False,
    )
```

profile of v0, /device:TPU:4, one launch (start us, length us, event | category | flops | bytes accessed | tf_op | source)
XLA Modules:
  0.0 932.4 jit_solution(7172400108618782772)
XLA Ops:
  7.9 0.7 all-gather.7.cloned.1.call-update
  8.7 83.6 %all-gather.5.cloned.1.call-done = f32[2048,128]{1,0:T(8,128)} async-done(((f32[128,128]{1,0:T(8,128)}), f32[2048,128]{1,0:T(8,128)}) %all-gather.5.cloned.1.call-update) | async-done | bytes 1048592 | tf_op jit(solution)/shard_map/all_gather | solution.py:58
  92.3 32.1 %all-gather.7.cloned.1.call-done = f32[2048,128]{1,0:T(8,128)} async-done(((f32[128,128]{1,0:T(8,128)}), f32[2048,128]{1,0:T(8,128)}) %all-gather.7.cloned.1.call-update) | async-done | bytes 1048592 | tf_op jit(solution)/shard_map/all_gather | solution.py:59
  124.6 71.9 %while.24 = (s32[]{:T(128)}, f32[2048,128]{1,0:T(8,128)S(1)}, f32[2048,128]{1,0:T(8,128)S(1)}, s32[6]{0:T(128)S(1)}, s32[3,1,1,6]{3,2,1,0:T(1,128)}, /*index=5*/...) while((s32[]{:T(128)}, f32[2048,128]{1,0:T(8,128)S(1)}, ...), condition=%wide.region_1.2_spmd, body=%wide.region_0.1_spmd.sunk | while | flops 604667904 | bytes 5456283 | solution.py:52
  127.1 1.3 constant_dynamic-slice_fusion.18
  129.6 0.9 constant_dynamic-slice_fusion.19
  131.9 1.1 dynamic-slice_convert_fusion.4
  134.9 1.0 fusion.52
  139.1 1.3 constant_dynamic-slice_fusion.18
  141.6 0.9 constant_dynamic-slice_fusion.19
  143.9 1.1 dynamic-slice_convert_fusion.4
  146.9 1.0 fusion.52
  151.1 1.3 constant_dynamic-slice_fusion.18
  153.6 0.9 constant_dynamic-slice_fusion.19
  155.9 1.1 dynamic-slice_convert_fusion.4
  158.8 1.0 fusion.52
  163.1 1.3 constant_dynamic-slice_fusion.18
  165.6 0.9 constant_dynamic-slice_fusion.19
  167.1 0.7 constant_dynamic-slice_fusion.20
  167.9 1.1 dynamic-slice_convert_fusion.4
  170.8 1.0 fusion.52
  175.1 1.3 constant_dynamic-slice_fusion.18
  177.6 0.9 constant_dynamic-slice_fusion.19
  179.8 1.1 dynamic-slice_convert_fusion.4
  182.8 1.0 fusion.52
  187.1 1.3 constant_dynamic-slice_fusion.18
  189.6 0.9 constant_dynamic-slice_fusion.19
  191.1 0.7 constant_dynamic-slice_fusion.20
  191.8 1.1 dynamic-slice_convert_fusion.4
  194.8 1.0 fusion.52
  196.6 1.0 copy-done.3
  198.2 58.2 %reduce-scatter.7.cloned.1.call-done = f32[128,128]{1,0:T(8,128)} async-done(((f32[2048,128]{1,0:T(8,128)}), f32[128,128]{1,0:T(8,128)}) %reduce-scatter.7.cloned.1.call-update) | async-done | bytes 65552 | tf_op jit(solution)/shard_map/reduce_scatter | solution.py:64
  256.4 1.5 multiply_subtract_fusion.2
  258.0 211.8 %reduce-scatter.5.cloned.1.call-done = f32[128,128]{1,0:T(8,128)} async-done(((f32[2048,128]{1,0:T(8,128)}), f32[128,128]{1,0:T(8,128)}) %reduce-scatter.5.cloned.1.call-update) | async-done | bytes 65552 | tf_op jit(solution)/shard_map/reduce_scatter | solution.py:63
  469.8 1.5 multiply_subtract_fusion.3
  471.4 32.5 %all-gather.11.cloned.1.call-done = f32[2048,128]{1,0:T(8,128)} async-done(((f32[128,128]{1,0:T(8,128)}), f32[2048,128]{1,0:T(8,128)}) %all-gather.11.cloned.1.call-update) | async-done | bytes 1048592 | tf_op jit(solution)/shard_map/all_gather | solution.py:59
  503.9 82.6 %all-gather.9.cloned.1.call-done = f32[2048,128]{1,0:T(8,128)} async-done(((f32[128,128]{1,0:T(8,128)}), f32[2048,128]{1,0:T(8,128)}) %all-gather.9.cloned.1.call-update) | async-done | bytes 1048592 | tf_op jit(solution)/shard_map/all_gather | solution.py:58
  586.7 68.0 %while.25 = (s32[]{:T(128)}, f32[2048,128]{1,0:T(8,128)S(1)}, f32[2048,128]{1,0:T(8,128)S(1)}, s32[6]{0:T(128)S(1)}, s32[3,1,1,6]{3,2,1,0:T(1,128)S(1)}, /*index...) while((s32[]{:T(128)}, f32[2048,128]{1,0:T(8,128)S(1)}, ...), condition=%wide.region_5.6_spmd, body=%wide.region_4.5_spmd.sunk | while | flops 604667904 | bytes 5456283 | solution.py:52
  591.1 0.9 constant_dynamic-slice_fusion.22
  592.7 0.7 constant_dynamic-slice_fusion.23
  593.4 1.1 dynamic-slice_convert_fusion.5
  596.4 1.0 fusion.61
  602.5 0.9 constant_dynamic-slice_fusion.22
  604.0 0.7 constant_dynamic-slice_fusion.23
  604.7 1.1 dynamic-slice_convert_fusion.5
  607.7 1.0 fusion.61
  613.8 0.9 constant_dynamic-slice_fusion.22
  616.1 1.1 dynamic-slice_convert_fusion.5
  619.0 1.0 fusion.61
  625.1 0.9 constant_dynamic-slice_fusion.22
  627.4 1.1 dynamic-slice_convert_fusion.5
  630.4 1.0 fusion.61
  636.5 0.9 constant_dynamic-slice_fusion.22
  638.7 1.1 dynamic-slice_convert_fusion.5
  641.7 1.0 fusion.61
  647.8 0.9 constant_dynamic-slice_fusion.22
  649.3 0.7 constant_dynamic-slice_fusion.23
  650.1 1.1 dynamic-slice_convert_fusion.5
  653.0 1.0 fusion.61
  654.8 0.9 copy-done.1
  656.5 53.7 %reduce-scatter.11.cloned.1.call-done = f32[128,128]{1,0:T(8,128)} async-done(((f32[2048,128]{1,0:T(8,128)}), f32[128,128]{1,0:T(8,128)}) %reduce-scatter.11.cloned.1.call-update) | async-done | bytes 65552 | tf_op jit(solution)/shard_map/reduce_scatter | solution.py:64
  710.2 1.5 multiply_subtract_fusion
  711.7 212.4 %reduce-scatter.9.cloned.1.call-done = f32[128,128]{1,0:T(8,128)} async-done(((f32[2048,128]{1,0:T(8,128)}), f32[128,128]{1,0:T(8,128)}) %reduce-scatter.9.cloned.1.call-update) | async-done | bytes 65552 | tf_op jit(solution)/shard_map/reduce_scatter | solution.py:63
  924.1 1.5 multiply_subtract_fusion.1
  (98 shorter events, 34.2 us)
Async XLA Ops:
  7.2 85.1 %all-gather.5.cloned.1.call-start = ((), (), s32[]{:S(2)}) async-start(), calls=%async_computation.4 | async-start | bytes 1114112 | tf_op jit(solution)/shard_map/all_gather | solution.py:58
  7.9 116.5 %all-gather.7.cloned.1.call-start = ((), (), s32[]{:S(2)}) async-start(), calls=%async_computation.5 | async-start | bytes 1114112 | tf_op jit(solution)/shard_map/all_gather | solution.py:59
  8.6 247.8 %reduce-scatter.7.cloned.1.call-start = ((), (), s32[]{:S(2)}) async-start(), calls=%async_computation.8 | async-start | bytes 1114112 | tf_op jit(solution)/shard_map/reduce_scatter | solution.py:64
  124.5 131.9 %copy-start.6 = (f32[128,128]{1,0:T(8,128)S(1)}, f32[128,128]{1,0:T(8,128)}, u32[]{:S(2)}) copy-start(f32[128,128]{1,0:T(8,128)} %param.14) | copy-start | bytes 196612
  124.6 345.2 %copy-start.7 = (f32[128,128]{1,0:T(8,128)S(1)}, f32[128,128]{1,0:T(8,128)}, u32[]{:S(2)}) copy-start(f32[128,128]{1,0:T(8,128)} %param.13) | copy-start | bytes 196612
  196.5 1.0 copy-start.3
  196.5 1.3 copy-start.2
  196.5 390.1 %copy-start.8 = (s32[3,1,1,6]{3,2,1,0:T(1,128)S(1)}, s32[3,1,1,6]{3,2,1,0:T(1,128)}, u32[]{:S(2)}) copy-start(s32[3,1,1,6]{3,2,1,0:T(1,128)} %get-tuple-element.431) | copy-start | bytes 220
  197.6 272.2 %reduce-scatter.5.cloned.1.call-start = ((), (), s32[]{:S(2)}) async-start(), calls=%async_computation.6 | async-start | bytes 1114112 | tf_op jit(solution)/shard_map/reduce_scatter | solution.py:63
  198.1 305.8 %all-gather.11.cloned.1.call-start = ((), (), s32[]{:S(2)}) async-start(), calls=%async_computation.9 | async-start | bytes 1114112 | tf_op jit(solution)/shard_map/all_gather | solution.py:59
  258.0 328.6 %all-gather.9.cloned.1.call-start = ((), (), s32[]{:S(2)}) async-start(), calls=%async_computation.7 | async-start | bytes 1114112 | tf_op jit(solution)/shard_map/all_gather | solution.py:58
  471.3 238.9 %reduce-scatter.11.cloned.1.call-start = ((), (), s32[]{:S(2)}) async-start(), calls=%async_computation.11 | async-start | bytes 1114112 | tf_op jit(solution)/shard_map/reduce_scatter | solution.py:64
  586.7 123.5 %copy-start.4 = (f32[128,128]{1,0:T(8,128)S(1)}, f32[128,128]{1,0:T(8,128)}, u32[]{:S(2)}) copy-start(f32[128,128]{1,0:T(8,128)} %multiply_subtract_fusion.2) | copy-start | bytes 196612
  586.7 337.3 %copy-start.5 = (f32[128,128]{1,0:T(8,128)S(1)}, f32[128,128]{1,0:T(8,128)}, u32[]{:S(2)}) copy-start(f32[128,128]{1,0:T(8,128)} %multiply_subtract_fusion.3) | copy-start | bytes 196612
  654.7 0.9 copy-start.1
  654.8 1.3 copy-start
  655.7 268.3 %reduce-scatter.9.cloned.1.call-start = ((), (), s32[]{:S(2)}) async-start(), calls=%async_computation.10 | async-start | bytes 1114112 | tf_op jit(solution)/shard_map/reduce_scatter | solution.py:63
Sparse Core Ops, SparseCore 0:
  10.6 81.6 all-gather.4
  94.1 30.2 all-gather.6
  197.7 58.7 reduce-scatter.6
  260.1 209.6 reduce-scatter.4
  472.1 31.7 all-gather.10
  506.9 79.5 all-gather.8
  655.8 54.2 reduce-scatter.10
  714.0 210.0 reduce-scatter.8
where the time goes:
time: 935 us; the launch traced here: 932 us
  waiting for transfers between devices  769 us (82%)
  loops' own time  61 us (7%)
  local copies, waits for them, and re-layouts  40.9 us (4%)
  matrix products  27.4 us (3%)
  other arithmetic  19.4 us (2%)
  between operations  14.3 us (2%)
    reduce_scatter x2, waiting for transfers between devices, local(): share_a = lax.psum_scatter(grad_a, 'col', scatter_dimension=0, tiled=True)  424 us
    all_gather x2, waiting for transfers between devices, local(): band_a = lax.all_gather(factor_a, 'col', axis=0, tiled=True)  166 us
    reduce_scatter x2, waiting for transfers between devices, local(): share_b = lax.psum_scatter(grad_b, 'row', scatter_dimension=0, tiled=True)  112 us
    all_gather x2, waiting for transfers between devices, local(): band_b = lax.all_gather(factor_b, 'row', axis=0, tiled=True)  64.7 us
    another operation x2, loops' own time, local_gradients(): lax.scan(visit_slot, start, jnp.arange(slot_total, dtype=jnp.int32))  61 us
  transfers between devices with their start and end apart: 8, of which 8 were waited for; matrix products, arithmetic and copies ran while one was open for 0% of the time, Pallas kernels for 0%

commit v1 on v0

--- a/solution.py
+++ b/solution.py
@@ -56,7 +56,10 @@
 def local(counts, block_coords, block_count, factor_a, factor_b, factor_c):
     for step_index in range(STEPS):
         band_a = lax.all_gather(factor_a, "col", axis=0, tiled=True)
-        band_b = lax.all_gather(factor_b, "row", axis=0, tiled=True)
+        size = lax.axis_size("row")
+        blocks = jnp.stack([factor_b for _ in range(size)])
+        blocks = lax.all_to_all(blocks, "row", split_axis=0, concat_axis=0)
+        band_b = jnp.concatenate(blocks, axis=0)
         grad_a, grad_b = local_gradients(
             band_a, band_b, factor_c, counts, block_coords, block_count
         )

time: 935 us -> 865 us (0.925)
  waiting for transfers between devices: 769 us -> 680 us
  starting transfers between devices: 0.32 us -> 17.9 us
    all_gather x2 -> x0, waiting for transfers between devices: 64.7 us -> none  [local(): band_b = lax.all_gather(factor_b, 'row', axis=0, tiled=True)]
    all_gather x2, waiting for transfers between devices: 166 us -> 129 us  [local(): band_a = lax.all_gather(factor_a, 'col', axis=0, tiled=True)]
    all_to_all x0 -> x2, waiting for transfers between devices: none -> 26.2 us  [local(): blocks = lax.all_to_all(blocks, 'row', split_axis=0, concat_axis=0)]
    all_to_all x0 -> x2, starting transfers between devices: none -> 17.7 us  [local(): blocks = lax.all_to_all(blocks, 'row', split_axis=0, concat_axis=0)]
    reduce_scatter x2, waiting for transfers between devices: 424 us -> 412 us  [local(): share_a = lax.psum_scatter(grad_a, 'col', scatter_dimension=0, tiled=True)]
  transfers between devices with their start and end apart: 8 -> 8, of which waited for: 8 -> 8; matrix products, arithmetic and copies ran while one was open for 0% -> 1% of each run, Pallas kernels for 0% -> 0%
where the time goes in v1:
time: 865 us; the launch traced here: 862 us
  waiting for transfers between devices  680 us (79%)
  loops' own time  63.8 us (7%)
  local copies, waits for them, and re-layouts  40.1 us (5%)
  matrix products  27.3 us (3%)
  other arithmetic  18.8 us (2%)
  starting transfers between devices  17.9 us (2%)
  between operations  14.2 us (2%)
    reduce_scatter x2, waiting for transfers between devices, local(): share_a = lax.psum_scatter(grad_a, 'col', scatter_dimension=0, tiled=True)  412 us
    all_gather x2, waiting for transfers between devices, local(): band_a = lax.all_gather(factor_a, 'col', axis=0, tiled=True)  129 us
    reduce_scatter x2, waiting for transfers between devices, local(): share_b = lax.psum_scatter(grad_b, 'row', scatter_dimension=0, tiled=True)  111 us
    another operation x2, loops' own time, local_gradients(): lax.scan(visit_slot, start, jnp.arange(slot_total, dtype=jnp.int32))  63.8 us
    all_to_all x2, waiting for transfers between devices, local(): blocks = lax.all_to_all(blocks, 'row', split_axis=0, concat_axis=0)  26.2 us
    all_to_all x2, starting transfers between devices, local(): blocks = lax.all_to_all(blocks, 'row', split_axis=0, concat_axis=0)  17.7 us
  transfers between devices with their start and end apart: 8, of which 8 were waited for; matrix products, arithmetic and copies ran while one was open for 1% of the time, Pallas kernels for 0%

profile of v1, /device:TPU:4, one launch (start us, length us, event | category | flops | bytes accessed | tf_op | source)
XLA Modules:
  0.0 861.8 jit_solution(87827882730778424)
XLA Ops:
  7.9 1.9 stack.4
  9.8 6.3 all-to-all-start
  16.2 13.1 %all-to-all-done = f32[16,128,128]{2,1,0:T(8,128)} async-done(((f32[16,128,128]{2,1,0:T(8,128)}), f32[16,128,128]{2,1,0:T(8,128)}, u32[]{:S(2)}, u32[]{:S(2)}) %all-to-all-start) | async-done | bytes 1048608 | tf_op jit(solution)/shard_map/all_to_all | solution.py:61
  29.3 65.0 %all-gather.3.cloned.1.call-done = f32[2048,128]{1,0:T(8,128)} async-done(((f32[128,128]{1,0:T(8,128)}), f32[2048,128]{1,0:T(8,128)}) %all-gather.3.cloned.1.call-update) | async-done | bytes 1048592 | tf_op jit(solution)/shard_map/all_gather | solution.py:58
  94.4 69.1 %while.24 = (s32[]{:T(128)}, f32[2048,128]{1,0:T(8,128)S(1)}, f32[2048,128]{1,0:T(8,128)S(1)}, s32[6]{0:T(128)S(1)}, s32[3,1,1,6]{3,2,1,0:T(1,128)S(1)}, /*index...) while((s32[]{:T(128)}, f32[2048,128]{1,0:T(8,128)S(1)}, ...), condition=%wide.region_1.2_spmd, body=%wide.region_0.1_spmd.sunk | while | flops 604667904 | bytes 5456283 | solution.py:52
  98.9 0.9 constant_dynamic-slice_fusion.19
  100.5 0.7 constant_dynamic-slice_fusion.20
  101.2 1.1 dynamic-slice_convert_fusion.4
  104.2 1.0 fusion.52
  110.4 0.9 constant_dynamic-slice_fusion.19
  112.0 0.7 constant_dynamic-slice_fusion.20
  112.8 1.1 dynamic-slice_convert_fusion.4
  115.7 1.0 fusion.52
  121.9 0.9 constant_dynamic-slice_fusion.19
  123.5 0.7 constant_dynamic-slice_fusion.20
  124.3 1.1 dynamic-slice_convert_fusion.4
  127.3 1.0 fusion.52
  133.5 0.9 constant_dynamic-slice_fusion.19
  135.0 0.7 constant_dynamic-slice_fusion.20
  135.8 1.1 dynamic-slice_convert_fusion.4
  138.8 1.0 fusion.52
  145.0 0.9 constant_dynamic-slice_fusion.19
  146.6 0.7 constant_dynamic-slice_fusion.20
  147.3 1.1 dynamic-slice_convert_fusion.4
  150.3 1.0 fusion.52
  156.5 0.9 constant_dynamic-slice_fusion.19
  158.1 0.7 constant_dynamic-slice_fusion.20
  158.8 1.1 dynamic-slice_convert_fusion.4
  161.8 1.0 fusion.52
  163.5 1.0 copy-done.2
  165.3 200.0 %reduce-scatter.5.cloned.1.call-done = f32[128,128]{1,0:T(8,128)} async-done(((f32[2048,128]{1,0:T(8,128)}), f32[128,128]{1,0:T(8,128)}) %reduce-scatter.5.cloned.1.call-update) | async-done | bytes 65552 | tf_op jit(solution)/shard_map/reduce_scatter | solution.py:66
  365.3 1.5 multiply_subtract_fusion.3
  366.8 57.0 %reduce-scatter.7.cloned.1.call-done = f32[128,128]{1,0:T(8,128)} async-done(((f32[2048,128]{1,0:T(8,128)}), f32[128,128]{1,0:T(8,128)}) %reduce-scatter.7.cloned.1.call-update) | async-done | bytes 65552 | tf_op jit(solution)/shard_map/reduce_scatter | solution.py:67
  423.8 0.9 multiply_subtract_fusion.2
  424.7 1.1 stack.5
  425.7 11.4 %all-to-all-start.1 = ((f32[16,128,128]{2,1,0:T(8,128)}), f32[16,128,128]{2,1,0:T(8,128)}, u32[]{:S(2)}, u32[]{:S(2)}) async-start(f32[16,128,128]{2,1,0:T(8,128)} %stack.5), calls=%async_computation.3 | async-start | bytes 2097152 | tf_op jit(solution)/shard_map/all_to_all | solution.py:61
  437.2 13.1 %all-to-all-done.1 = f32[16,128,128]{2,1,0:T(8,128)} async-done(((f32[16,128,128]{2,1,0:T(8,128)}), f32[16,128,128]{2,1,0:T(8,128)}, u32[]{:S(2)}, u32[]{:S(2)}) %all-to-all-start.1) | async-done | bytes 1048608 | tf_op jit(solution)/shard_map/all_to_all | solution.py:61
  450.3 64.0 %all-gather.5.cloned.1.call-done = f32[2048,128]{1,0:T(8,128)} async-done(((f32[128,128]{1,0:T(8,128)}), f32[2048,128]{1,0:T(8,128)}) %all-gather.5.cloned.1.call-update) | async-done | bytes 1048592 | tf_op jit(solution)/shard_map/all_gather | solution.py:58
  514.5 69.8 %while.25 = (s32[]{:T(128)}, f32[2048,128]{1,0:T(8,128)S(1)}, f32[2048,128]{1,0:T(8,128)S(1)}, s32[6]{0:T(128)S(1)}, s32[3,1,1,6]{3,2,1,0:T(1,128)S(1)}, /*index...) while((s32[]{:T(128)}, f32[2048,128]{1,0:T(8,128)S(1)}, ...), condition=%wide.region_5.6_spmd, body=%wide.region_4.5_spmd.sunk | while | flops 604667904 | bytes 5456283 | solution.py:52
  519.1 0.9 constant_dynamic-slice_fusion.22
  521.4 1.1 dynamic-slice_convert_fusion.5
  524.4 1.0 fusion.61
  530.8 0.9 constant_dynamic-slice_fusion.22
  532.3 0.7 constant_dynamic-slice_fusion.23
  533.0 1.1 dynamic-slice_convert_fusion.5
  536.1 1.0 fusion.61
  542.4 0.9 constant_dynamic-slice_fusion.22
  544.7 1.1 dynamic-slice_convert_fusion.5
  547.7 1.0 fusion.61
  554.1 0.9 constant_dynamic-slice_fusion.22
  555.6 0.7 constant_dynamic-slice_fusion.23
  556.3 1.1 dynamic-slice_convert_fusion.5
  559.4 1.0 fusion.61
  565.7 0.9 constant_dynamic-slice_fusion.22
  568.0 1.1 dynamic-slice_convert_fusion.5
  571.0 1.0 fusion.61
  577.3 0.9 constant_dynamic-slice_fusion.22
  579.6 1.1 dynamic-slice_convert_fusion.5
  582.6 1.0 fusion.61
  584.4 1.0 copy-done.1
  585.9 53.9 %reduce-scatter.11.cloned.1.call-done = f32[128,128]{1,0:T(8,128)} async-done(((f32[2048,128]{1,0:T(8,128)}), f32[128,128]{1,0:T(8,128)}) %reduce-scatter.11.cloned.1.call-update) | async-done | bytes 65552 | tf_op jit(solution)/shard_map/reduce_scatter | solution.py:67
  639.8 1.5 multiply_subtract_fusion
  641.3 212.2 %reduce-scatter.9.cloned.1.call-done = f32[128,128]{1,0:T(8,128)} async-done(((f32[2048,128]{1,0:T(8,128)}), f32[128,128]{1,0:T(8,128)}) %reduce-scatter.9.cloned.1.call-update) | async-done | bytes 65552 | tf_op jit(solution)/shard_map/reduce_scatter | solution.py:66
  853.5 1.5 multiply_subtract_fusion.1
  (96 shorter events, 36.1 us)
Async XLA Ops:
  7.2 87.2 %copy-start.7 = (s32[3,1,1,6]{3,2,1,0:T(1,128)S(1)}, s32[3,1,1,6]{3,2,1,0:T(1,128)}, u32[]{:S(2)}) copy-start(s32[3,1,1,6]{3,2,1,0:T(1,128)} %param.11) | copy-start | bytes 220
  7.2 87.1 %all-gather.3.cloned.1.call-start = ((), (), s32[]{:S(2)}) async-start(), calls=%async_computation.6 | async-start | bytes 1114112 | tf_op jit(solution)/shard_map/all_gather | solution.py:58
  9.8 19.4 %all-to-all-start = ((f32[16,128,128]{2,1,0:T(8,128)}), f32[16,128,128]{2,1,0:T(8,128)}, u32[]{:S(2)}, u32[]{:S(2)}) async-start(f32[16,128,128]{2,1,0:T(8,128)} %stack.4), calls=%async_computation | async-start | bytes 2097152 | tf_op jit(solution)/shard_map/all_to_all | solution.py:61
  16.1 349.2 %reduce-scatter.5.cloned.1.call-start = ((), (), s32[]{:S(2)}) async-start(), calls=%async_computation.7 | async-start | bytes 1114112 | tf_op jit(solution)/shard_map/reduce_scatter | solution.py:66
  94.4 270.9 %copy-start.6 = (f32[128,128]{1,0:T(8,128)S(1)}, f32[128,128]{1,0:T(8,128)}, u32[]{:S(2)}) copy-start(f32[128,128]{1,0:T(8,128)} %param.13) | copy-start | bytes 196612
  94.4 329.4 %copy-start.5 = (f32[128,128]{1,0:T(8,128)S(1)}, f32[128,128]{1,0:T(8,128)}, u32[]{:S(2)}) copy-start(f32[128,128]{1,0:T(8,128)} %param.14) | copy-start | bytes 196612
  163.5 1.0 copy-start.2
  163.5 1.3 copy-start.3
  164.5 259.3 %reduce-scatter.7.cloned.1.call-start = ((), (), s32[]{:S(2)}) async-start(), calls=%async_computation.9 | async-start | bytes 1114112 | tf_op jit(solution)/shard_map/reduce_scatter | solution.py:67
  165.3 349.1 %all-gather.5.cloned.1.call-start = ((), (), s32[]{:S(2)}) async-start(), calls=%async_computation.8 | async-start | bytes 1114112 | tf_op jit(solution)/shard_map/all_gather | solution.py:58
  425.7 24.5 %all-to-all-start.1 = ((f32[16,128,128]{2,1,0:T(8,128)}), f32[16,128,128]{2,1,0:T(8,128)}, u32[]{:S(2)}, u32[]{:S(2)}) async-start(f32[16,128,128]{2,1,0:T(8,128)} %stack.5), calls=%async_computation.3 | async-start | bytes 2097152 | tf_op jit(solution)/shard_map/all_to_all | solution.py:61
  437.2 202.6 %reduce-scatter.11.cloned.1.call-start = ((), (), s32[]{:S(2)}) async-start(), calls=%async_computation.11 | async-start | bytes 1114112 | tf_op jit(solution)/shard_map/reduce_scatter | solution.py:67
  514.5 339.0 %copy-start.4 = (f32[128,128]{1,0:T(8,128)S(1)}, f32[128,128]{1,0:T(8,128)}, u32[]{:S(2)}) copy-start(f32[128,128]{1,0:T(8,128)} %multiply_subtract_fusion.3) | copy-start | bytes 196612
  584.3 1.0 copy-start.1
  584.3 1.3 copy-start
  585.3 268.1 %reduce-scatter.9.cloned.1.call-start = ((), (), s32[]{:S(2)}) async-start(), calls=%async_computation.10 | async-start | bytes 1114112 | tf_op jit(solution)/shard_map/reduce_scatter | solution.py:66
Sparse Core Ops, SparseCore 0:
  10.6 83.6 all-gather.2
  164.6 200.6 reduce-scatter.4
  367.8 55.9 reduce-scatter.6
  426.8 87.4 all-gather.4
  585.5 54.2 reduce-scatter.10
  643.5 209.9 reduce-scatter.8
